TPU v7x, 32 devices: a whole 2x2x4 slice. The times are simulated.
32 devices in a mesh: ctx: 2 (over y), fsdp: 16 (over z, x, core).
Axes of the slice: x: 2, y: 2, z: 4, core: 2. Of those that a mesh axis runs over, the one named last changes fastest.
Arguments:
- tokens: bfloat16 [16, 1024, 768], P('fsdp', 'ctx'), may hold values from -6 to 6
- step_embed: bfloat16 [16, 768], P('fsdp'), may hold values from -3 to 3
- block_ids: int32 [16, 4], P('fsdp', 'ctx'), may hold values from 0 to 3, as said below
- cotangent: bfloat16 [16, 1024, 768], P('fsdp', 'ctx'), may hold values from -6 to 6
- project_weight: float32 [768, 2304], P('fsdp'), may hold values from -0.21875 to 0.21875
- project_bias: float32 [2, 768], P(None, 'fsdp'), may hold values from -2 to 2
- output_weight: float32 [768, 768], P('fsdp'), may hold values from -3 to 3
- output_bias: float32 [768], P('fsdp'), may hold values from -2 to 2
- first_gain: float32 [768], P('fsdp'), may hold values from 0.25 to 1.75
- first_shift: float32 [768], P('fsdp'), may hold values from -2 to 2
- up_weight: float32 [768, 3072], P('fsdp'), may hold values from -0.21875 to 0.21875
- up_bias: float32 [3072], P('fsdp'), may hold values from -3 to 3
- down_weight: float32 [3072, 768], P('fsdp'), may hold values from -0.109375 to 0.109375
- down_bias: float32 [768], P('fsdp'), may hold values from -2 to 2
- second_gain: float32 [768], P('fsdp'), may hold values from 0.25 to 1.75
- second_shift: float32 [768], P('fsdp'), may hold values from -2 to 2
Outputs:
- output: float32 [16, 1024, 768], P('fsdp', 'ctx')
- token_grad: float32 [16, 1024, 768], P('fsdp', 'ctx')
- grad_project_weight: float32 [768, 2304], P('fsdp')
- grad_project_bias: float32 [2, 768], P(None, 'fsdp')
- grad_output_weight: float32 [768, 768], P('fsdp')
- grad_output_bias: float32 [768], P('fsdp')
- grad_first_gain: float32 [768], P('fsdp')
- grad_first_shift: float32 [768], P('fsdp')
- grad_up_weight: float32 [768, 3072], P('fsdp')
- grad_up_bias: float32 [3072], P('fsdp')
- grad_down_weight: float32 [3072, 768], P('fsdp')
- grad_down_bias: float32 [768], P('fsdp')
- grad_second_gain: float32 [768], P('fsdp')
- grad_second_shift: float32 [768], P('fsdp')
Inputs may be any that keep to these rules, and one draw needn't show every extreme that they name: `block_ids`: in every sequence each id appears once, and the two blocks stored on one index of ctx have ids adding to 3.
All inputs are finite; a program needn't handle non-finite values.
Results may differ from a plain program's by a relative error of at most 0.019.
The roundings to bfloat16 on the way count: a program that leaves them out, or rounds other values in their place, can miss the bound.
Values may be sent and summed in bfloat16 or wider, within the bound.
No kernel may reach another device: no remote copies, remote signals or barrier semaphores. Data moves between devices by JAX's collectives and lax.ppermute only.
A program may use at most 192 MiB of HBM per device.

v0:
```python
import jax
import jax.numpy as jnp
from jax import lax
from jax.sharding import PartitionSpec as P

HEADS = 12
norm_epsilon = 1e-05
masked_score = -1e30


def layer_norm(values, gain, shift):
    center = values - jnp.mean(values, axis=-1, keepdims=True)
    spread = jnp.mean(center * center, axis=-1, keepdims=True)
    return center * lax.rsqrt(spread + norm_epsilon) * gain + shift


def gelu_exact(values):
    return jax.nn.gelu(values, approximate=False)


def product(left, right):
    return jnp.dot(left, right, preferred_element_type=jnp.float32)


def transpose_left(left, right):
    return lax.dot_general(
        left, right, (((0,), (0,)), ((), ())), preferred_element_type=jnp.float32
    )


def transpose_right(left, right):
    return lax.dot_general(
        left, right, (((1,), (1,)), ((), ())), preferred_element_type=jnp.float32
    )


def column_sum(values):
    return jnp.sum(values.astype(jnp.float32), axis=0)


def shards(
    tokens,
    step_embed,
    block_ids,
    cotangent,
    project_weight,
    project_bias,
    output_weight,
    output_bias,
    first_gain,
    first_shift,
    up_weight,
    up_bias,
    down_weight,
    down_bias,
    second_gain,
    second_shift,
):
    gathered = (
        lax.all_gather(project_weight.astype(jnp.bfloat16), "fsdp", axis=0, tiled=True),
        lax.all_gather(project_bias.astype(jnp.bfloat16), "fsdp", axis=1, tiled=True),
        lax.all_gather(output_weight.astype(jnp.bfloat16), "fsdp", axis=0, tiled=True),
        lax.all_gather(output_bias.astype(jnp.bfloat16), "fsdp", axis=0, tiled=True),
        lax.all_gather(first_gain.astype(jnp.bfloat16), "fsdp", axis=0, tiled=True),
        lax.all_gather(first_shift.astype(jnp.bfloat16), "fsdp", axis=0, tiled=True),
        lax.all_gather(up_weight.astype(jnp.bfloat16), "fsdp", axis=0, tiled=True),
        lax.all_gather(up_bias.astype(jnp.bfloat16), "fsdp", axis=0, tiled=True),
        lax.all_gather(down_weight.astype(jnp.bfloat16), "fsdp", axis=0, tiled=True),
        lax.all_gather(down_bias.astype(jnp.bfloat16), "fsdp", axis=0, tiled=True),
        lax.all_gather(second_gain.astype(jnp.bfloat16), "fsdp", axis=0, tiled=True),
        lax.all_gather(second_shift.astype(jnp.bfloat16), "fsdp", axis=0, tiled=True),
    )
    (
        project_matrix,
        project_offset,
        output_matrix,
        output_offset,
        first_scale,
        first_offset,
        up_matrix,
        up_offset,
        down_matrix,
        down_offset,
        second_scale,
        second_offset,
    ) = gathered
    seq_count, pair_rows, width = tokens.shape
    head_dim = width // HEADS
    pair_width = 2 * head_dim
    pair_count = HEADS // 2
    scale = head_dim ** (-0.5)
    flat_rows = seq_count * pair_rows
    pair_indices = jnp.arange(pair_count, dtype=jnp.int32)

    def head_pair(source, pair_index):
        piece = lax.dynamic_slice_in_dim(source, pair_index * pair_width, pair_width, 2)
        return piece.reshape(seq_count, source.shape[1], 2, head_dim)

    def merge_pairs(stacked):
        return jnp.transpose(stacked, (1, 2, 0, 3)).reshape(flat_rows, width)

    hidden_zero = (tokens.astype(jnp.float32) + step_embed.astype(jnp.float32)[:, None, :]).reshape(
        flat_rows, width
    )
    hidden_zero_low = hidden_zero.astype(jnp.bfloat16)
    offsets = project_offset.astype(jnp.float32)
    bias_row = jnp.concatenate([offsets[0], jnp.zeros_like(offsets[0]), offsets[1]])
    projected = (product(hidden_zero_low, project_matrix) + bias_row).astype(jnp.bfloat16)
    queries = projected[:, :width].reshape(seq_count, pair_rows, width)
    keys_here = projected[:, width : 2 * width].reshape(seq_count, pair_rows, width)
    values_here = projected[:, 2 * width :].reshape(seq_count, pair_rows, width)
    keys_all, values_all, ids_all = (
        lax.all_gather(keys_here, "ctx", axis=1, tiled=True),
        lax.all_gather(values_here, "ctx", axis=1, tiled=True),
        lax.all_gather(block_ids.astype(jnp.bfloat16), "ctx", axis=1, tiled=True),
    )
    block_rows = pair_rows // block_ids.shape[1]
    query_ids = jnp.repeat(block_ids, block_rows, axis=1)
    key_ids = jnp.repeat(ids_all.astype(jnp.int32), block_rows, axis=1)
    allowed = key_ids[:, None, None, :] <= query_ids[:, None, :, None]

    def forward_pair(pair_index):
        query_pair = head_pair(queries, pair_index)
        key_pair = head_pair(keys_all, pair_index)
        value_pair = head_pair(values_all, pair_index)
        scores = (
            jnp.einsum("bqhd,bkhd->bhqk", query_pair, key_pair, preferred_element_type=jnp.float32)
            * scale
        )
        scores = jnp.where(allowed, scores, masked_score)
        peak = jnp.max(scores, axis=-1, keepdims=True)
        expon = jnp.exp(scores - peak)
        totals = jnp.sum(expon, axis=-1, keepdims=True)
        probs = expon / totals
        mixed_pair = jnp.einsum(
            "bhqk,bkhd->bqhd",
            probs.astype(jnp.bfloat16),
            value_pair,
            preferred_element_type=jnp.float32,
        )
        log_total = (peak + jnp.log(totals))[..., 0]
        return (
            mixed_pair.astype(jnp.bfloat16).reshape(seq_count, pair_rows, pair_width),
            log_total,
        )

    mixed_pairs, log_totals = lax.map(forward_pair, pair_indices)
    mixed = merge_pairs(mixed_pairs)
    branch = product(mixed, output_matrix) + output_offset.astype(jnp.float32)
    hidden_one, first_pull = jax.vjp(
        layer_norm,
        hidden_zero + branch,
        first_scale.astype(jnp.float32),
        first_offset.astype(jnp.float32),
    )
    hidden_one_low = hidden_one.astype(jnp.bfloat16)
    inner = product(hidden_one_low, up_matrix) + up_offset.astype(jnp.float32)
    activated, gelu_pull = jax.vjp(gelu_exact, inner)
    activated_low = activated.astype(jnp.bfloat16)
    feed = product(activated_low, down_matrix) + down_offset.astype(jnp.float32)
    result, second_pull = jax.vjp(
        layer_norm,
        hidden_one + feed,
        second_scale.astype(jnp.float32),
        second_offset.astype(jnp.float32),
    )
    project_back, output_back, up_back, down_back = (
        lax.all_gather(project_weight.astype(jnp.bfloat16), "fsdp", axis=0, tiled=True),
        lax.all_gather(output_weight.astype(jnp.bfloat16), "fsdp", axis=0, tiled=True),
        lax.all_gather(up_weight.astype(jnp.bfloat16), "fsdp", axis=0, tiled=True),
        lax.all_gather(down_weight.astype(jnp.bfloat16), "fsdp", axis=0, tiled=True),
    )
    grad_second_in, grad_second_gain, grad_second_shift = second_pull(
        cotangent.reshape(flat_rows, width).astype(jnp.float32)
    )
    feed_grad = grad_second_in.astype(jnp.bfloat16)
    grad_down_bias = column_sum(feed_grad)
    grad_down_weight = transpose_left(activated_low, feed_grad)
    activated_grad = transpose_right(feed_grad, down_back)
    inner_grad = gelu_pull(activated_grad)[0].astype(jnp.bfloat16)
    grad_up_bias = column_sum(inner_grad)
    grad_up_weight = transpose_left(hidden_one_low, inner_grad)
    hidden_one_grad = grad_second_in + transpose_right(inner_grad, up_back)
    grad_first_in, grad_first_gain, grad_first_shift = first_pull(hidden_one_grad)
    branch_grad = grad_first_in.astype(jnp.bfloat16)
    grad_output_bias = column_sum(branch_grad)
    grad_output_weight = transpose_left(mixed, branch_grad)
    mixed_grad = (
        transpose_right(branch_grad, output_back)
        .astype(jnp.bfloat16)
        .reshape(seq_count, pair_rows, width)
    )

    def backward_pair(pair_inputs):
        pair_index, log_total = pair_inputs
        query_pair = head_pair(queries, pair_index)
        key_pair = head_pair(keys_all, pair_index)
        value_pair = head_pair(values_all, pair_index)
        grad_pair = head_pair(mixed_grad, pair_index)
        scores = (
            jnp.einsum("bqhd,bkhd->bhqk", query_pair, key_pair, preferred_element_type=jnp.float32)
            * scale
        )
        probs = jnp.where(allowed, jnp.exp(scores - log_total[..., None]), 0.0)
        prob_grad = jnp.einsum(
            "bqhd,bkhd->bhqk", grad_pair, value_pair, preferred_element_type=jnp.float32
        )
        row_dot = jnp.sum(probs * prob_grad, axis=-1, keepdims=True)
        score_grad = (probs * (prob_grad - row_dot)).astype(jnp.bfloat16)
        query_grad = (
            jnp.einsum("bhqk,bkhd->bqhd", score_grad, key_pair, preferred_element_type=jnp.float32)
            * scale
        )
        key_grad = (
            jnp.einsum(
                "bhqk,bqhd->bkhd", score_grad, query_pair, preferred_element_type=jnp.float32
            )
            * scale
        )
        value_grad = jnp.einsum(
            "bhqk,bqhd->bkhd",
            probs.astype(jnp.bfloat16),
            grad_pair,
            preferred_element_type=jnp.float32,
        )
        return (
            query_grad.astype(jnp.bfloat16).reshape(seq_count, pair_rows, pair_width),
            key_grad.reshape(seq_count, key_pair.shape[1], pair_width),
            value_grad.reshape(seq_count, key_pair.shape[1], pair_width),
        )

    query_grads, key_partial, value_partial = lax.map(backward_pair, (pair_indices, log_totals))
    key_sums, value_sums = (
        lax.psum_scatter(
            key_partial.astype(jnp.bfloat16), "ctx", scatter_dimension=2, tiled=True
        ).astype(jnp.float32),
        lax.psum_scatter(
            value_partial.astype(jnp.bfloat16), "ctx", scatter_dimension=2, tiled=True
        ).astype(jnp.float32),
    )
    key_grads = key_sums.astype(jnp.bfloat16)
    value_grads = value_sums.astype(jnp.bfloat16)
    project_grad = jnp.concatenate(
        [merge_pairs(query_grads), merge_pairs(key_grads), merge_pairs(value_grads)], axis=1
    )
    grad_project_bias = jnp.stack(
        [column_sum(project_grad[:, :width]), column_sum(project_grad[:, 2 * width :])]
    )
    grad_project_weight = transpose_left(hidden_zero_low, project_grad)
    input_grad = grad_first_in + transpose_right(project_grad, project_back)
    shares = (
        lax.psum_scatter(
            grad_project_weight.astype(jnp.bfloat16), "fsdp", scatter_dimension=0, tiled=True
        ).astype(jnp.float32),
        lax.psum_scatter(
            grad_project_bias.astype(jnp.bfloat16), "fsdp", scatter_dimension=1, tiled=True
        ).astype(jnp.float32),
        lax.psum_scatter(
            grad_output_weight.astype(jnp.bfloat16), "fsdp", scatter_dimension=0, tiled=True
        ).astype(jnp.float32),
        lax.psum_scatter(
            grad_output_bias.astype(jnp.bfloat16), "fsdp", scatter_dimension=0, tiled=True
        ).astype(jnp.float32),
        lax.psum_scatter(
            grad_first_gain.astype(jnp.bfloat16), "fsdp", scatter_dimension=0, tiled=True
        ).astype(jnp.float32),
        lax.psum_scatter(
            grad_first_shift.astype(jnp.bfloat16), "fsdp", scatter_dimension=0, tiled=True
        ).astype(jnp.float32),
        lax.psum_scatter(
            grad_up_weight.astype(jnp.bfloat16), "fsdp", scatter_dimension=0, tiled=True
        ).astype(jnp.float32),
        lax.psum_scatter(
            grad_up_bias.astype(jnp.bfloat16), "fsdp", scatter_dimension=0, tiled=True
        ).astype(jnp.float32),
        lax.psum_scatter(
            grad_down_weight.astype(jnp.bfloat16), "fsdp", scatter_dimension=0, tiled=True
        ).astype(jnp.float32),
        lax.psum_scatter(
            grad_down_bias.astype(jnp.bfloat16), "fsdp", scatter_dimension=0, tiled=True
        ).astype(jnp.float32),
        lax.psum_scatter(
            grad_second_gain.astype(jnp.bfloat16), "fsdp", scatter_dimension=0, tiled=True
        ).astype(jnp.float32),
        lax.psum_scatter(
            grad_second_shift.astype(jnp.bfloat16), "fsdp", scatter_dimension=0, tiled=True
        ).astype(jnp.float32),
    )
    summed = (
        lax.psum(shares[0].astype(jnp.bfloat16), "ctx").astype(jnp.float32),
        lax.psum(shares[1].astype(jnp.bfloat16), "ctx").astype(jnp.float32),
        lax.psum(shares[2].astype(jnp.bfloat16), "ctx").astype(jnp.float32),
        lax.psum(shares[3].astype(jnp.bfloat16), "ctx").astype(jnp.float32),
        lax.psum(shares[4].astype(jnp.bfloat16), "ctx").astype(jnp.float32),
        lax.psum(shares[5].astype(jnp.bfloat16), "ctx").astype(jnp.float32),
        lax.psum(shares[6].astype(jnp.bfloat16), "ctx").astype(jnp.float32),
        lax.psum(shares[7].astype(jnp.bfloat16), "ctx").astype(jnp.float32),
        lax.psum(shares[8].astype(jnp.bfloat16), "ctx").astype(jnp.float32),
        lax.psum(shares[9].astype(jnp.bfloat16), "ctx").astype(jnp.float32),
        lax.psum(shares[10].astype(jnp.bfloat16), "ctx").astype(jnp.float32),
        lax.psum(shares[11].astype(jnp.bfloat16), "ctx").astype(jnp.float32),
    )
    return (
        result.reshape(seq_count, pair_rows, width),
        input_grad.reshape(seq_count, pair_rows, width),
        summed[0],
        summed[1],
        summed[2],
        summed[3],
        summed[4],
        summed[5],
        summed[6],
        summed[7],
        summed[8],
        summed[9],
        summed[10],
        summed[11],
    )


def solution(mesh):
    return jax.shard_map(
        shards,
        mesh=mesh,
        in_specs=(
            P("fsdp", "ctx", None),
            P("fsdp", None),
            P("fsdp", "ctx"),
            P("fsdp", "ctx", None),
            P("fsdp", None),
            P(None, "fsdp"),
            P("fsdp", None),
            P("fsdp"),
            P("fsdp"),
            P("fsdp"),
            P("fsdp", None),
            P("fsdp"),
            P("fsdp", None),
            P("fsdp"),
            P("fsdp"),
            P("fsdp"),
        ),
        out_specs=(
            P("fsdp", "ctx", None),
            P("fsdp", "ctx", None),
            P("fsdp", None),
            P(None, "fsdp"),
            P("fsdp", None),
            P("fsdp"),
            P("fsdp"),
            P("fsdp"),
            P("fsdp", None),
            P("fsdp"),
            P("fsdp", None),
            P("fsdp"),
            P("fsdp"),
            P("fsdp"),
        ),
        check_vma=False,
    )
```

profile of v0, /device:TPU:0, one launch (start us, length us, event | category | flops | bytes accessed | tf_op | source)
XLA Modules:
  0.0 857.9 jit_solution(12785414366772415956)
XLA Ops:
  7.2 1.7 convert_element_type.245
  9.7 23.0 %all-gather.2 = bf16[16,48,2]{1,2,0:T(2,128)(2,1)S(1)} all-gather(bf16[1,48,2]{1,2,0:T(2,128)(2,1)S(1)} %convert_bitcast_fusion.1), channel_id=1, replica_groups=mesh['ctx'=2,'fsdp'=16] {'fsdp'}, dimensions={0}, use_global_device_ids=true | all-gather | bytes 3264 | tf_op jit(solution)/shard_map/all_gather | solution.py:61
  33.5 27.3 %all-gather.10.cloned.1.call-done = bf16[768,2304]{1,0:T(8,128)(2,1)} async-done(((bf16[48,2304]{1,0:T(8,128)(2,1)}), bf16[768,2304]{1,0:T(8,128)(2,1)}) %all-gather.10.cloned.1.call-update) | async-done | bytes 3538960 | tf_op jit(solution)/shard_map/all_gather | solution.py:60
  60.8 4.3 fusion.23
  74.6 59.6 %all-reduce.16 = (bf16[768]{0:T(1024)(128)(2,1)S(1)}, bf16[768]{0:T(1024)(128)(2,1)S(1)}, bf16[768]{0:T(1024)(128)(2,1)S(1)}, bf16[3072]{0:T(1024)(128)(2,1)S(1)...) all-reduce(bf16[768]{0:T(1024)(128)(2,1)S(1)} %dynamic-update-slice, ...), channel_id=1, replica_groups=mesh['ctx'=2,'fsdp'=16] {'fsdp'}, use_global_device_ids=true, to_apply=%add.1 | all-reduce | flops 6912 | bytes 27648
  134.2 5.2 all-reduce
  140.8 1.7 copy.54
  142.6 1.7 copy.56
  145.3 41.9 %while.28 = (s32[]{:T(128)}, bf16[6,1,512,128]{2,3,1,0:T(8,128)(2,1)}, f32[6,1,2,512]{3,2,1,0:T(2,128)S(1)}, s32[6]{0:T(128)S(1)}, bf16[1,1024,768]{1,2,0:T(8,12...) while((s32[]{:T(128)}, ...), condition=%wide.region_3.4_spmd.clone, body=%wide.region_0.3_spmd.clone.sunk | while | flops 281607168 | bytes 17078980 | solution.py:147
  150.1 1.5 fusion.102
  157.1 1.5 fusion.102
  164.1 1.5 fusion.102
  171.1 1.5 fusion.102
  178.1 1.5 fusion.102
  185.1 1.5 fusion.102
  187.2 3.2 fusion.45
  191.9 26.7 %all-gather.14.cloned.1.call-done = bf16[768,3072]{1,0:T(8,128)(2,1)} async-done(((bf16[48,3072]{1,0:T(8,128)(2,1)}), bf16[768,3072]{1,0:T(8,128)(2,1)}) %all-gather.14.cloned.1.call-update) | async-done | bytes 4718608 | tf_op jit(solution)/shard_map/all_gather | solution.py:66
  218.6 21.3 %multiply_convert_fusion.1 = (bf16[512,3072]{1,0:T(8,128)(2,1)}, f32[512,3072]{1,0:T(8,128)}, f32[512,3072]{1,0:T(8,128)}) fusion(f32[3072]{0:T(1024)S(1)} %convert_element_type.262, bf16[768,3072]{1,0:T(8,128)(2,1)} %all-gather.14.cloned.1.call-done, f32[512,768]{1,0:T(8,128)} %copy-done.8, f32[768]{0:T(1024)S(1)} %convert_element_type.258, ...), kind=kOutput, calls=%fused_computation.40 | convolution fusion | flops 2521694208 | bytes 22042624 | tf_op jit(solution)/shard_map/dot_general | solution.py:22
  240.0 33.4 %all-gather.16.cloned.1.call-done = bf16[3072,768]{1,0:T(8,128)(2,1)} async-done(((bf16[192,768]{1,0:T(8,128)(2,1)}), bf16[3072,768]{1,0:T(8,128)(2,1)}) %all-gather.16.cloned.1.call-update) | async-done | bytes 4718608 | tf_op jit(solution)/shard_map/all_gather | solution.py:68
  273.3 6.5 fusion.46
  281.9 1.7 copy-done.20
  283.6 9.2 %fusion.38 = (bf16[3072]{0:T(1024)(128)(2,1)S(1)}, bf16[512,3072]{1,0:T(8,128)(2,1)}) fusion(f32[512,3072]{1,0:T(8,128)} %get-tuple-element.341, f32[512,3072]{1,0:T(8,128)} %get-tuple-element.357, f32[3072]{0:T(1024)S(1)} %convert_element_type.262, bf16[512,768]{1,0:T(8,128)(2,1)S(1)} %get-tuple-element.331, bf16[3072,768]{1,0:T(8,128)(2,1)S(1)} %copy-done.20), kind=kOutput, calls=%fused_computation.115 | convolution fusion | flops 2441081856 | bytes 21252096 | tf_op jit(solution)/shard_map/dot_general | solution.py:32
  292.8 5.1 multiply_reduce_fusion.1
  300.8 1.7 fusion.28
  303.6 101.8 %while.29 = (s32[]{:T(128)}, bf16[6,1,512,128]{2,3,1,0:T(8,128)(2,1)}, bf16[6,1,1024,128]{2,3,1,0:T(8,128)(2,1)}, bf16[6,1,1024,128]{2,3,1,0:T(8,128)(2,1)}, s32...) while((s32[]{:T(128)}, ...), condition=%wide.region_14.15_spmd.clone, body=%wide.region_12.14_spmd.clone.sunk | while | flops 687733760 | bytes 68062520 | solution.py:232
  306.0 2.7 fusion.113
  311.1 4.1 multiply_reduce_fusion.6
  315.2 1.4 multiply_convert_fusion.3
  323.0 2.7 fusion.113
  328.1 4.1 multiply_reduce_fusion.6
  332.2 1.4 multiply_convert_fusion.3
  339.9 2.7 fusion.113
  345.0 4.1 multiply_reduce_fusion.6
  349.1 1.4 multiply_convert_fusion.3
  356.9 2.7 fusion.113
  361.9 4.1 multiply_reduce_fusion.6
  366.1 1.4 multiply_convert_fusion.3
  373.8 2.7 fusion.113
  378.9 4.1 multiply_reduce_fusion.6
  383.0 1.4 multiply_convert_fusion.3
  390.7 2.7 fusion.113
  395.8 4.1 multiply_reduce_fusion.6
  400.0 1.4 multiply_convert_fusion.3
  406.2 3.2 convolution_convert_fusion.3
  409.5 7.0 convolution_convert_fusion
  416.6 1.3 copy-done.10
  417.9 6.5 convolution_convert_fusion.1
  424.7 5.5 reduce-scatter.12.cloned.1.call-done
  430.2 29.0 %reduce-scatter.10.cloned.1.call-done = bf16[6,1,512,128]{2,3,1,0:T(8,128)(2,1)} async-done(((bf16[6,1,1024,128]{2,3,1,0:T(8,128)(2,1)}), bf16[6,1,512,128]{2,3,1,0:T(8,128)(2,1)}) %reduce-scatter.10.cloned.1.call-update) | async-done | bytes 786448 | tf_op jit(solution)/shard_map/reduce_scatter | solution.py:234
  459.2 5.4 convolution_convert_fusion.2
  464.7 1.4 bitcast_reduce_fusion.1
  469.2 61.3 %all-reduce.15 = (bf16[768]{0:T(1024)(128)(2,1)S(1)}, bf16[768]{0:T(1024)(128)(2,1)S(1)}, bf16[768]{0:T(1024)(128)(2,1)S(1)}, bf16[768]{0:T(1024)(128)(2,1)S(1)}...) all-reduce(bf16[768]{0:T(1024)(128)(2,1)S(1)} %dynamic-update-slice, ...), channel_id=1, replica_groups=mesh['ctx'=2,'fsdp'=16] {'fsdp'}, use_global_device_ids=true, to_apply=%add.7 | all-reduce | flops 8448 | bytes 33792
  531.0 68.3 %reduce-scatter.20.cloned.1.call-done = bf16[192,768]{1,0:T(8,128)(2,1)} async-done(((bf16[3072,768]{1,0:T(8,128)(2,1)}), bf16[192,768]{1,0:T(8,128)(2,1)}) %reduce-scatter.20.cloned.1.call-update) | async-done | bytes 294928 | tf_op jit(solution)/shard_map/reduce_scatter | solution.py:276
  599.3 79.1 %reduce-scatter.18.cloned.1.call-done = bf16[48,3072]{1,0:T(8,128)(2,1)} async-done(((bf16[768,3072]{1,0:T(8,128)(2,1)}), bf16[48,3072]{1,0:T(8,128)(2,1)}) %reduce-scatter.18.cloned.1.call-update) | async-done | bytes 294928 | tf_op jit(solution)/shard_map/reduce_scatter | solution.py:270
  678.4 70.8 %reduce-scatter.14.cloned.1.call-done = bf16[48,2304]{1,0:T(8,128)(2,1)} async-done(((bf16[768,2304]{1,0:T(8,128)(2,1)}), bf16[48,2304]{1,0:T(8,128)(2,1)}) %reduce-scatter.14.cloned.1.call-update) | async-done | bytes 221200 | tf_op jit(solution)/shard_map/reduce_scatter | solution.py:252
  749.2 1.4 add_bitcast_fusion.1
  750.7 5.9 add_bitcast_fusion
  756.6 49.2 %reduce-scatter.22.cloned.1.call-done = bf16[48,2]{1,0:T(8,128)(2,1)} async-done(((bf16[768,2]{1,0:T(8,128)(2,1)}), bf16[48,2]{1,0:T(8,128)(2,1)}) %reduce-scatter.22.cloned.1.call-update) | async-done | bytes 208
  806.6 4.9 all-reduce.17
  815.7 28.5 %all-reduce.21.cloned.1.call-done = (bf16[48,2304]{1,0:T(8,128)(2,1)}, bf16[48,768]{1,0:T(8,128)(2,1)}, bf16[48,3072]{1,0:T(8,128)(2,1)}, bf16[192,768]{1,0:T(8,128)(2,1)}) async-done(((bf16[48,2304]{1,0:T(8,128)(2,1)}, bf16[48,768]{1,0:T(8,128)(2,1)}, bf16[48,3072]{1,0:T(8,128)(2,1)}, bf16[192,768]{1,0:T(8,128)(2,1)}), (bf16[48,2304]{1,0:T(8,128)(2,1)}, bf16[48,768]{1,0:T(8,128)(2,1)}, ...) | async-done | bytes 884752 | tf_op jit(solution)/shard_map/psum | solution.py:290
  844.3 1.8 convert_element_type.292
  846.1 1.8 convert_element_type.295
  847.9 1.7 convert_element_type.280
  849.6 1.6 convert_element_type.285
  (346 shorter events, 104.1 us)
Async XLA Ops:
  7.2 53.6 %all-gather.10.cloned.1.call-start = ((), (), s32[]{:S(2)}) async-start(), calls=%async_computation.7 | async-start | bytes 3760128 | tf_op jit(solution)/shard_map/all_gather | solution.py:60
  9.0 131.9 %all-gather.18.cloned.1.call-start = ((), (), s32[]{:S(2)}) async-start(), calls=%async_computation.17 | async-start | bytes 2359296 | tf_op jit(solution)/shard_map/all_gather | solution.py:114
  65.0 2.3 copy-start.17
  65.1 3.0 copy-start.15
  65.1 3.8 copy-start.16
  65.1 4.7 copy-start.24
  65.1 4.7 copy-start.25
  65.1 4.7 copy-start.26
  65.1 4.7 copy-start.27
  65.1 4.7 copy-start.28
  65.1 4.7 copy-start.18
  65.2 6.6 copy-start.23
  65.2 6.6 copy-start.30
  65.2 7.2 copy-start.19
  66.5 76.0 %all-gather.20.cloned.1.call-start = ((), (), s32[]{:S(2)}) async-start(), calls=%async_computation.18 | async-start | bytes 2359296 | tf_op jit(solution)/shard_map/all_gather | solution.py:113
  67.3 120.0 %all-gather.12.cloned.1.call-start = ((), (), s32[]{:S(2)}) async-start(), calls=%async_computation.8 | async-start | bytes 1253376 | tf_op jit(solution)/shard_map/all_gather | solution.py:62
  68.0 150.6 %all-gather.14.cloned.1.call-start = ((), (), s32[]{:S(2)}) async-start(), calls=%async_computation.9 | async-start | bytes 5013504 | tf_op jit(solution)/shard_map/all_gather | solution.py:66
  68.8 204.5 %all-gather.16.cloned.1.call-start = ((), (), s32[]{:S(2)}) async-start(), calls=%async_computation.10 | async-start | bytes 5013504 | tf_op jit(solution)/shard_map/all_gather | solution.py:68
  69.7 360.5 %reduce-scatter.12.cloned.1.call-start = ((), (), s32[]{:S(2)}) async-start(), calls=%async_computation.12 | async-start | bytes 2359296 | tf_op jit(solution)/shard_map/reduce_scatter | solution.py:237
  187.2 4.7 copy-start.1
  190.5 1.1 copy-start.8
  273.3 6.9 copy-start.4
  280.9 2.6 copy-start.20
  281.6 11.1 %slice-start = ((s8[4718592]{0:T(1024)(128)(4,1)}), s8[4194304]{0:T(1024)(128)(4,1)S(1)}, s32[]{:S(2)}) async-start(s8[4718592]{0:T(1024)(128)(4,1)} %bitcast.216), calls=%async_computation.21 | async-start | bytes 8388608
  281.9 10.9 %copy-start.12 = (bf16[512,768]{1,0:T(8,128)(2,1)}, bf16[512,768]{1,0:T(8,128)(2,1)S(1)}, u32[]{:S(2)}) copy-start(bf16[512,768]{1,0:T(8,128)(2,1)S(1)} %get-tuple-element.331) | copy-start | bytes 2359300
  283.6 9.2 %copy-start.9 = (f32[512,768]{1,0:T(8,128)S(1)}, f32[512,768]{1,0:T(8,128)}, u32[]{:S(2)}) copy-start(f32[512,768]{1,0:T(8,128)} %copy-done.8) | copy-start | bytes 4718596
  283.6 9.2 %slice-start.1 = ((s8[4718592]{0:T(1024)(128)(4,1)}), s8[524288]{0:T(1024)(128)(4,1)S(1)}, s32[]{:S(2)}) async-start(s8[4718592]{0:T(1024)(128)(4,1)} %bitcast.216), calls=%async_computation.22 | async-start | bytes 1048576
  297.9 2.9 copy-start.21
  298.6 1.2 copy-start.6
  300.0 0.9 copy-start.14
  303.7 1.4 copy-start.2
  311.1 4.1 copy-start
  318.4 2.3 copy-start.3
  320.7 1.4 copy-start.2
  328.0 4.1 copy-start
  335.3 2.3 copy-start.3
  337.6 1.4 copy-start.2
  345.0 4.1 copy-start
  352.3 2.3 copy-start.3
  354.6 1.4 copy-start.2
  361.9 4.1 copy-start
  369.2 2.3 copy-start.3
  371.5 1.4 copy-start.2
  378.9 4.1 copy-start
  386.2 2.3 copy-start.3
  388.4 1.4 copy-start.2
  395.8 4.1 copy-start
  403.1 2.3 copy-start.3
  405.4 4.1 copy-start.13
  405.4 53.8 %reduce-scatter.10.cloned.1.call-start = ((), (), s32[]{:S(2)}) async-start(), calls=%async_computation.11 | async-start | bytes 2359296 | tf_op jit(solution)/shard_map/reduce_scatter | solution.py:234
  406.2 124.8 %reduce-scatter.16.cloned.1.call-start = ((), (), s32[]{:S(2)}) async-start(), calls=%async_computation.14 | async-start | bytes 1253376 | tf_op jit(solution)/shard_map/reduce_scatter | solution.py:258
  409.4 189.9 %reduce-scatter.20.cloned.1.call-start = ((), (), s32[]{:S(2)}) async-start(), calls=%async_computation.16 | async-start | bytes 5013504 | tf_op jit(solution)/shard_map/reduce_scatter | solution.py:276
  416.5 1.4 copy-start.10
  416.5 261.8 %reduce-scatter.18.cloned.1.call-start = ((), (), s32[]{:S(2)}) async-start(), calls=%async_computation.15 | async-start | bytes 5013504 | tf_op jit(solution)/shard_map/reduce_scatter | solution.py:270
  424.4 34.8 %copy-start.22 = (bf16[1,512,768]{2,1,0:T(8,128)(2,1)S(1)}, bf16[1,512,768]{2,1,0:T(8,128)(2,1)}, u32[]{:S(2)}) copy-start(bf16[1,512,768]{2,1,0:T(8,128)(2,1)} %param.20) | copy-start | bytes 2359300
  424.5 324.8 %reduce-scatter.14.cloned.1.call-start = ((), (), s32[]{:S(2)}) async-start(), calls=%async_computation.13 | async-start | bytes 3760128 | tf_op jit(solution)/shard_map/reduce_scatter | solution.py:252
  464.7 1.5 copy-start.11
  464.7 2.7 copy-start.29
  464.7 2.7 copy-start.5
  464.7 341.1 %reduce-scatter.22.cloned.1.call-start = ((), (), s32[]{:S(2)}) async-start(), calls=%async_computation.19 | async-start | bytes 208896
  467.3 377.0 %all-reduce.21.cloned.1.call-start = ((), (), s32[]{:S(2)}) async-start(), calls=%async_computation.20 | async-start | bytes 1769472 | tf_op jit(solution)/shard_map/psum | solution.py:290
  467.5 283.2 %copy-start.7 = (f32[512,768]{1,0:T(8,128)S(1)}, f32[512,768]{1,0:T(8,128)}, u32[]{:S(2)}) copy-start(f32[512,768]{1,0:T(8,128)} %copy-done.6) | copy-start | bytes 4718596
Sparse Core Ops, SparseCore 0:
  10.9 49.8 all-gather.9
  66.7 26.2 all-gather.17
  95.0 27.2 all-gather.19
  125.0 38.3 all-gather.11
  166.2 52.4 all-gather.13
  221.4 51.9 all-gather.15
  405.5 24.6 reduce-scatter.11
  433.1 26.0 reduce-scatter.9
  462.8 58.0 reduce-scatter.15
  524.7 74.5 reduce-scatter.19
  603.6 74.6 reduce-scatter.17
  682.1 67.0 reduce-scatter.13
  753.3 52.4 reduce-scatter.21
  808.2 36.0 all-reduce.20
where the time goes:
time: 864 us; the launch traced here: 858 us
  waiting for transfers between devices  419 us (48%)
  blocking collectives  154 us (18%)
  matrix products  151 us (17%)
  local copies, waits for them, and re-layouts  63.7 us (7%)
  other arithmetic  42.3 us (5%)
  between operations  18.2 us (2%)
  loops' own time  8.76 us (1%)
    unnamed x3, blocking collectives  126 us
    reduce_scatter x1, waiting for transfers between devices, shards(): lax.psum_scatter(grad_up_weight.astype(jnp.bfloat16), 'fsdp', scatter_dim...  79.1 us
    reduce_scatter x1, waiting for transfers between devices, shards(): lax.psum_scatter(grad_project_weight.astype(jnp.bfloat16), 'fsdp', scatte...  70.8 us
    reduce_scatter x1, waiting for transfers between devices, shards(): lax.psum_scatter(grad_down_weight.astype(jnp.bfloat16), 'fsdp', scatter_d...  68.3 us
    unnamed x15, waiting for transfers between devices  50.8 us
    dot_general x4, matrix products, product(): return jnp.dot(left, right, preferred_element_type=jnp.float32)  35.3 us
    all_gather x1, waiting for transfers between devices, shards(): lax.all_gather(down_weight.astype(jnp.bfloat16), 'fsdp', axis=0, tiled=True)  33.4 us
    reduce_scatter x1, waiting for transfers between devices, shards(): lax.psum_scatter(key_partial.astype(jnp.bfloat16), 'ctx', scatter_dimensi...  29 us
  transfers between devices with their start and end apart: 14, of which 10 were waited for; matrix products, arithmetic and copies ran while one was open for 13% of the time, Pallas kernels for 0%

commit v1 on v0

--- a/solution.py
+++ b/solution.py
@@ -6,6 +6,11 @@
 HEADS = 12
 norm_epsilon = 1e-05
 masked_score = -1e30
+
+
+def summed_here(shard, mesh_axis):
+    blocks = lax.all_gather(shard, mesh_axis)
+    return jnp.sum(blocks, axis=0)
 
 
 def layer_norm(values, gain, shift):
@@ -287,7 +292,7 @@
         ).astype(jnp.float32),
     )
     summed = (
-        lax.psum(shares[0].astype(jnp.bfloat16), "ctx").astype(jnp.float32),
+        summed_here(shares[0].astype(jnp.bfloat16), "ctx").astype(jnp.float32),
         lax.psum(shares[1].astype(jnp.bfloat16), "ctx").astype(jnp.float32),
         lax.psum(shares[2].astype(jnp.bfloat16), "ctx").astype(jnp.float32),
         lax.psum(shares[3].astype(jnp.bfloat16), "ctx").astype(jnp.float32),

time: 864 us -> 873 us (1.010)
  waiting for transfers between devices: 419 us -> 400 us
  local copies, waits for them, and re-layouts: 63.7 us -> 77.8 us
    reduce_scatter x1, waiting for transfers between devices: 0.01 us -> 60.3 us  [shards(): lax.psum_scatter(grad_output_weight.astype(jnp.bfloat16), 'fsdp', scatter...]
    unnamed x15, waiting for transfers between devices: 50.8 us -> 1.56 us
    psum x1, waiting for transfers between devices: 28.5 us -> 3.52 us  [shards(): lax.psum(shares[2].astype(jnp.bfloat16), 'ctx').astype(jnp.float32)]
    all_gather x1, waiting for transfers between devices: 26.7 us -> 16 us  [shards(): lax.all_gather(up_weight.astype(jnp.bfloat16), 'fsdp', axis=0, tiled=True)]
    reduce_scatter x1, waiting for transfers between devices: 68.3 us -> 78.3 us  [shards(): lax.psum_scatter(grad_down_weight.astype(jnp.bfloat16), 'fsdp', scatter_d...]
  transfers between devices with their start and end apart: 14 -> 14, of which waited for: 10 -> 10; matrix products, arithmetic and copies ran while one was open for 13% -> 15% of each run, Pallas kernels for 0% -> 0%
where the time goes in v1:
time: 873 us; the launch traced here: 866 us
  waiting for transfers between devices  400 us (46%)
  blocking collectives  161 us (18%)
  matrix products  151 us (17%)
  local copies, waits for them, and re-layouts  77.8 us (9%)
  other arithmetic  48.7 us (6%)
  between operations  18.1 us (2%)
    unnamed x3, blocking collectives  126 us
    reduce_scatter x1, waiting for transfers between devices, shards(): lax.psum_scatter(grad_up_weight.astype(jnp.bfloat16), 'fsdp', scatter_dim...  79 us
    reduce_scatter x1, waiting for transfers between devices, shards(): lax.psum_scatter(grad_down_weight.astype(jnp.bfloat16), 'fsdp', scatter_d...  78.3 us
    reduce_scatter x1, waiting for transfers between devices, shards(): lax.psum_scatter(grad_project_weight.astype(jnp.bfloat16), 'fsdp', scatte...  67.3 us
    reduce_scatter x1, waiting for transfers between devices, shards(): lax.psum_scatter(grad_output_weight.astype(jnp.bfloat16), 'fsdp', scatter...  60.3 us
    all_gather x1, waiting for transfers between devices, shards(): lax.all_gather(down_weight.astype(jnp.bfloat16), 'fsdp', axis=0, tiled=True)  34.4 us
    dot_general x4, matrix products, product(): return jnp.dot(left, right, preferred_element_type=jnp.float32)  33.6 us
    dynamic_slice x42, local copies, waits for them, and re-layouts, head_pair(): lax.dynamic_slice_in_dim(source, pair_index * pair_width, pair_width, 2)  29.2 us
  transfers between devices with their start and end apart: 14, of which 10 were waited for; matrix products, arithmetic and copies ran while one was open for 15% of the time, Pallas kernels for 0%

profile of v1, /device:TPU:0, one launch (start us, length us, event | category | flops | bytes accessed | tf_op | source)
XLA Modules:
  0.0 866.2 jit_solution(2566838862846077224)
XLA Ops:
  7.2 1.7 convert_element_type.247
  9.7 23.0 %all-gather.3 = bf16[16,48,2]{1,2,0:T(2,128)(2,1)S(1)} all-gather(bf16[1,48,2]{1,2,0:T(2,128)(2,1)S(1)} %convert_bitcast_fusion.1), channel_id=1, replica_groups=mesh['ctx'=2,'fsdp'=16] {'fsdp'}, dimensions={0}, use_global_device_ids=true | all-gather | bytes 3264 | tf_op jit(solution)/shard_map/all_gather | solution.py:66
  33.5 27.2 %all-gather.11.cloned.1.call-done = bf16[768,2304]{1,0:T(8,128)(2,1)} async-done(((bf16[48,2304]{1,0:T(8,128)(2,1)}), bf16[768,2304]{1,0:T(8,128)(2,1)}) %all-gather.11.cloned.1.call-update) | async-done | bytes 3538960 | tf_op jit(solution)/shard_map/all_gather | solution.py:65
  60.8 4.3 fusion.23
  68.0 1.8 convert_element_type.262
  69.9 1.8 convert_element_type.266
  75.1 59.7 %all-reduce.16 = (bf16[768]{0:T(1024)(128)(2,1)S(1)}, bf16[768]{0:T(1024)(128)(2,1)S(1)}, bf16[768]{0:T(1024)(128)(2,1)S(1)}, bf16[3072]{0:T(1024)(128)(2,1)S(1)...) all-reduce(bf16[768]{0:T(1024)(128)(2,1)S(1)} %dynamic-update-slice, ...), channel_id=1, replica_groups=mesh['ctx'=2,'fsdp'=16] {'fsdp'}, use_global_device_ids=true, to_apply=%add.1 | all-reduce | flops 6912 | bytes 27648
  136.4 5.2 all-reduce
  142.9 2.6 copy.54
  145.5 1.7 copy.56
  148.2 51.1 %while.28 = (s32[]{:T(128)}, bf16[6,1,512,128]{2,3,1,0:T(8,128)(2,1)}, f32[6,1,2,512]{3,2,1,0:T(2,128)}, s32[6]{0:T(128)S(1)}, bf16[1,1024,768]{1,2,0:T(8,128)(2...) while((s32[]{:T(128)}, ...), condition=%wide.region_3.4_spmd.clone, body=%wide.region_0.3_spmd.clone.sunk | while | flops 281607168 | bytes 17078480 | solution.py:152
  154.0 1.5 fusion.102
  162.5 1.5 fusion.102
  171.0 1.5 fusion.102
  179.6 1.5 fusion.102
  188.1 1.5 fusion.102
  196.6 1.5 fusion.102
  199.4 2.7 fusion.45
  202.4 16.0 %all-gather.15.cloned.1.call-done = bf16[768,3072]{1,0:T(8,128)(2,1)} async-done(((bf16[48,3072]{1,0:T(8,128)(2,1)}), bf16[768,3072]{1,0:T(8,128)(2,1)}) %all-gather.15.cloned.1.call-update) | async-done | bytes 4718608 | tf_op jit(solution)/shard_map/all_gather | solution.py:71
  218.4 20.1 %multiply_convert_fusion.1 = (bf16[512,3072]{1,0:T(8,128)(2,1)}, f32[512,3072]{1,0:T(8,128)}, f32[512,3072]{1,0:T(8,128)}) fusion(f32[3072]{0:T(1024)S(1)} %convert_element_type.264, bf16[768,3072]{1,0:T(8,128)(2,1)} %all-gather.15.cloned.1.call-done, f32[512,768]{1,0:T(8,128)S(1)} %get-tuple-element.355, f32[768]{0:T(1024)S(1)} %convert_element_type.260, ...), kind=kOutput, calls=%fused_computation.40 | convolution fusion | flops 2521694208 | bytes 22042624 | tf_op jit(solution)/shard_map/dot_general | solution.py:27
  238.5 34.4 %all-gather.17.cloned.1.call-done = bf16[3072,768]{1,0:T(8,128)(2,1)} async-done(((bf16[192,768]{1,0:T(8,128)(2,1)}), bf16[3072,768]{1,0:T(8,128)(2,1)}) %all-gather.17.cloned.1.call-update) | async-done | bytes 4718608 | tf_op jit(solution)/shard_map/all_gather | solution.py:73
  272.9 6.5 fusion.46
  283.4 10.0 %fusion.38 = (bf16[3072]{0:T(1024)(128)(2,1)}, bf16[512,3072]{1,0:T(8,128)(2,1)}) fusion(f32[512,3072]{1,0:T(8,128)} %get-tuple-element.340, f32[512,3072]{1,0:T(8,128)} %get-tuple-element.356, f32[3072]{0:T(1024)S(1)} %convert_element_type.264, bf16[512,768]{1,0:T(8,128)(2,1)S(1)} %get-tuple-element.330, bf16[3072,768]{1,0:T(8,128)(2,1)S(1)} %copy-done.38), kind=kOutput, calls=%fused_computation.115 | convolution fusion | flops 2441081856 | bytes 21252096 | tf_op jit(solution)/shard_map/dot_general | solution.py:37
  293.4 5.7 multiply_reduce_fusion.1
  302.7 1.7 fusion.28
  305.9 109.9 %while.29 = (s32[]{:T(128)}, bf16[6,1,512,128]{2,3,1,0:T(8,128)(2,1)}, bf16[6,1,1024,128]{2,3,1,0:T(8,128)(2,1)}, bf16[6,1,1024,128]{2,3,1,0:T(8,128)(2,1)}, s32...) while((s32[]{:T(128)}, ...), condition=%wide.region_14.15_spmd.clone, body=%wide.region_12.14_spmd.clone.sunk | while | flops 687733760 | bytes 68061512 | solution.py:237
  308.9 2.7 fusion.113
  314.7 4.1 multiply_reduce_fusion.6
  318.8 1.4 multiply_convert_fusion.3
  327.2 2.7 fusion.113
  333.0 4.1 multiply_reduce_fusion.6
  337.1 1.4 multiply_convert_fusion.3
  345.5 2.7 fusion.113
  351.3 4.1 multiply_reduce_fusion.6
  355.4 1.4 multiply_convert_fusion.3
  363.8 2.7 fusion.113
  369.6 4.1 multiply_reduce_fusion.6
  373.7 1.4 multiply_convert_fusion.3
  382.0 2.7 fusion.113
  387.8 4.1 multiply_reduce_fusion.6
  392.0 1.4 multiply_convert_fusion.3
  400.3 2.7 fusion.113
  406.1 4.1 multiply_reduce_fusion.6
  410.3 1.4 multiply_convert_fusion.3
  415.9 3.3 convolution_convert_fusion.3
  419.3 7.0 convolution_convert_fusion.1
  427.4 6.8 convolution_convert_fusion
  435.5 5.1 reduce-scatter.12.cloned.1.call-done
  440.6 1.3 bitcast_reduce_fusion
  442.9 60.3 %reduce-scatter.16.cloned.1.call-done = bf16[48,768]{1,0:T(8,128)(2,1)} async-done(((bf16[768,768]{1,0:T(8,128)(2,1)}), bf16[48,768]{1,0:T(8,128)(2,1)}) %reduce-scatter.16.cloned.1.call-update) | async-done | bytes 73744 | tf_op jit(solution)/shard_map/reduce_scatter | solution.py:263
  503.2 79.0 %reduce-scatter.18.cloned.1.call-done = bf16[48,3072]{1,0:T(8,128)(2,1)} async-done(((bf16[768,3072]{1,0:T(8,128)(2,1)}), bf16[48,3072]{1,0:T(8,128)(2,1)}) %reduce-scatter.18.cloned.1.call-update) | async-done | bytes 294928 | tf_op jit(solution)/shard_map/reduce_scatter | solution.py:275
  582.2 78.3 %reduce-scatter.20.cloned.1.call-done = bf16[192,768]{1,0:T(8,128)(2,1)} async-done(((bf16[3072,768]{1,0:T(8,128)(2,1)}), bf16[192,768]{1,0:T(8,128)(2,1)}) %reduce-scatter.20.cloned.1.call-update) | async-done | bytes 294928 | tf_op jit(solution)/shard_map/reduce_scatter | solution.py:281
  660.8 27.2 %reduce-scatter.10.cloned.1.call-done = bf16[6,1,512,128]{2,3,1,0:T(8,128)(2,1)} async-done(((bf16[6,1,1024,128]{2,3,1,0:T(8,128)(2,1)}), bf16[6,1,512,128]{2,3,1,0:T(8,128)(2,1)}) %reduce-scatter.10.cloned.1.call-update) | async-done | bytes 786448 | tf_op jit(solution)/shard_map/reduce_scatter | solution.py:239
  688.1 5.4 convolution_convert_fusion.2
  696.4 61.2 %all-reduce.15 = (bf16[768]{0:T(1024)(128)(2,1)S(1)}, bf16[768]{0:T(1024)(128)(2,1)S(1)}, bf16[768]{0:T(1024)(128)(2,1)S(1)}, bf16[768]{0:T(1024)(128)(2,1)S(1)}...) all-reduce(bf16[768]{0:T(1024)(128)(2,1)S(1)} %dynamic-update-slice, ...), channel_id=1, replica_groups=mesh['ctx'=2,'fsdp'=16] {'fsdp'}, use_global_device_ids=true, to_apply=%add.7 | all-reduce | flops 8448 | bytes 33792
  758.1 1.4 add_bitcast_fusion.1
  759.6 6.2 add_bitcast_fusion
  766.6 4.9 all-reduce.17
  775.7 3.5 all-reduce.21.cloned.1.call-done
  779.2 1.6 convert_element_type.287
  780.8 1.8 convert_element_type.294
  782.6 1.8 convert_element_type.297
  784.4 67.3 %reduce-scatter.14.cloned.1.call-done = bf16[48,2304]{1,0:T(8,128)(2,1)} async-done(((bf16[768,2304]{1,0:T(8,128)(2,1)}), bf16[48,2304]{1,0:T(8,128)(2,1)}) %reduce-scatter.14.cloned.1.call-update) | async-done | bytes 221200 | tf_op jit(solution)/shard_map/reduce_scatter | solution.py:257
  851.7 6.8 all-gather.2
  (382 shorter events, 125.0 us)
Async XLA Ops:
  7.2 53.6 %all-gather.11.cloned.1.call-start = ((), (), s32[]{:S(2)}) async-start(), calls=%async_computation.7 | async-start | bytes 3760128 | tf_op jit(solution)/shard_map/all_gather | solution.py:65
  9.0 134.0 %all-gather.19.cloned.1.call-start = ((), (), s32[]{:S(2)}) async-start(), calls=%async_computation.17 | async-start | bytes 2359296 | tf_op jit(solution)/shard_map/all_gather | solution.py:119
  33.5 165.8 %copy-start.30 = (f32[768]{0:T(1024)}, f32[768]{0:T(1024)S(1)}, u32[]{:S(2)}) copy-start(f32[768]{0:T(1024)S(1)} %convert_reduce_fusion) | copy-start | bytes 9220
  65.1 6.8 copy-start.41
  65.1 6.8 copy-start.42
  65.1 6.8 copy-start.43
  65.1 6.8 copy-start.40
  65.1 6.8 copy-start.36
  65.1 8.7 %copy-start.44 = (f32[48]{0:T(128)S(1)}, f32[48]{0:T(128)}, u32[]{:S(2)}) copy-start(f32[48]{0:T(128)} %param.33) | copy-start | bytes 580
  65.1 8.7 %copy-start.45 = (f32[48]{0:T(128)S(1)}, f32[48]{0:T(128)}, u32[]{:S(2)}) copy-start(f32[48]{0:T(128)} %param.34) | copy-start | bytes 580
  65.1 69.7 %copy-start.37 = (s32[1,2]{1,0:T(1,128)S(1)}, s32[1,2]{1,0:T(1,128)}, u32[]{:S(2)}) copy-start(s32[1,2]{1,0:T(1,128)} %param.22) | copy-start | bytes 28
  65.2 69.7 %copy-start.47 = (u32[32]{0:T(128)S(1)}, u32[32]{0:T(128)}, u32[]{:S(2)}) copy-start(u32[32]{0:T(128)} %constant.143) | copy-start | bytes 388
  66.5 79.0 %all-gather.21.cloned.1.call-start = ((), (), s32[]{:S(2)}) async-start(), calls=%async_computation.18 | async-start | bytes 2359296 | tf_op jit(solution)/shard_map/all_gather | solution.py:118
  67.2 132.1 %all-gather.13.cloned.1.call-start = ((), (), s32[]{:S(2)}) async-start(), calls=%async_computation.8 | async-start | bytes 1253376 | tf_op jit(solution)/shard_map/all_gather | solution.py:67
  67.9 150.4 %all-gather.15.cloned.1.call-start = ((), (), s32[]{:S(2)}) async-start(), calls=%async_computation.9 | async-start | bytes 5013504 | tf_op jit(solution)/shard_map/all_gather | solution.py:71
  69.8 203.1 %all-gather.17.cloned.1.call-start = ((), (), s32[]{:S(2)}) async-start(), calls=%async_computation.10 | async-start | bytes 5013504 | tf_op jit(solution)/shard_map/all_gather | solution.py:73
  71.7 368.9 %reduce-scatter.12.cloned.1.call-start = ((), (), s32[]{:S(2)}) async-start(), calls=%async_computation.12 | async-start | bytes 2359296 | tf_op jit(solution)/shard_map/reduce_scatter | solution.py:242
  141.7 131.2 %copy-start.32 = (f32[768]{0:T(1024)}, f32[768]{0:T(1024)S(1)}, u32[]{:S(2)}) copy-start(f32[768]{0:T(1024)S(1)} %convert_element_type.260) | copy-start | bytes 9220
  141.7 157.5 %copy-start.20 = (f32[768]{0:T(1024)}, f32[768]{0:T(1024)S(1)}, u32[]{:S(2)}) copy-start(f32[768]{0:T(1024)S(1)} %convert_element_type.258) | copy-start | bytes 9220
  202.0 36.5 %copy-start.6 = (f32[512,768]{1,0:T(8,128)}, f32[512,768]{1,0:T(8,128)S(1)}, u32[]{:S(2)}) copy-start(f32[512,768]{1,0:T(8,128)S(1)} %get-tuple-element.355) | copy-start | bytes 4718596
  202.0 97.1 %copy-start.18 = (f32[512]{0:T(512)}, f32[512]{0:T(512)S(1)}, u32[]{:S(2)}) copy-start(f32[512]{0:T(512)S(1)} %broadcast_multiply_fusion.1) | copy-start | bytes 6148
  202.4 96.8 %copy-start.27 = (f32[512]{0:T(512)}, f32[512]{0:T(512)S(1)}, u32[]{:S(2)}) copy-start(f32[512]{0:T(512)S(1)} %fusion.30) | copy-start | bytes 6148
  272.9 6.9 copy-start.3
  279.8 2.8 copy-start.16
  281.7 11.7 %slice-start = ((s8[4718592]{0:T(1024)(128)(4,1)}), s8[4194304]{0:T(1024)(128)(4,1)S(1)}, s32[]{:S(2)}) async-start(s8[4718592]{0:T(1024)(128)(4,1)} %bitcast.222), calls=%async_computation.21 | async-start | bytes 8388608
  282.5 10.9 %copy-start.10 = (bf16[512,768]{1,0:T(8,128)(2,1)}, bf16[512,768]{1,0:T(8,128)(2,1)S(1)}, u32[]{:S(2)}) copy-start(bf16[512,768]{1,0:T(8,128)(2,1)S(1)} %get-tuple-element.330) | copy-start | bytes 2359300
  283.4 10.1 %copy-start.7 = (f32[512,768]{1,0:T(8,128)S(1)}, f32[512,768]{1,0:T(8,128)}, u32[]{:S(2)}) copy-start(f32[512,768]{1,0:T(8,128)} %copy-done.6) | copy-start | bytes 4718596
  283.4 10.1 %slice-start.1 = ((s8[4718592]{0:T(1024)(128)(4,1)}), s8[524288]{0:T(1024)(128)(4,1)S(1)}, s32[]{:S(2)}) async-start(s8[4718592]{0:T(1024)(128)(4,1)} %bitcast.222), calls=%async_computation.22 | async-start | bytes 1048576
  299.2 3.5 copy-start.39
  299.9 4.5 copy-start.25
  306.0 6.3 copy-start.1
  314.7 4.1 copy-start
  324.3 6.2 copy-start.1
  333.0 4.1 copy-start
  342.6 6.2 copy-start.1
  351.3 4.1 copy-start
  360.9 6.2 copy-start.1
  369.5 4.1 copy-start
  379.2 6.2 copy-start.1
  387.8 4.1 copy-start
  397.5 6.2 copy-start.1
  406.1 4.1 copy-start
  415.8 3.4 copy-start.8
  415.8 3.4 copy-start.19
  415.8 3.5 copy-start.21
  415.8 3.5 copy-start.28
  415.8 3.5 copy-start.33
  415.8 87.4 %reduce-scatter.16.cloned.1.call-start = ((), (), s32[]{:S(2)}) async-start(), calls=%async_computation.14 | async-start | bytes 1253376 | tf_op jit(solution)/shard_map/reduce_scatter | solution.py:263
  419.2 163.0 %reduce-scatter.18.cloned.1.call-start = ((), (), s32[]{:S(2)}) async-start(), calls=%async_computation.15 | async-start | bytes 5013504 | tf_op jit(solution)/shard_map/reduce_scatter | solution.py:275
  426.3 234.3 %reduce-scatter.20.cloned.1.call-start = ((), (), s32[]{:S(2)}) async-start(), calls=%async_computation.16 | async-start | bytes 5013504 | tf_op jit(solution)/shard_map/reduce_scatter | solution.py:281
  434.2 253.9 %copy-start.31 = (f32[768]{0:T(1024)S(1)}, f32[768]{0:T(1024)}, u32[]{:S(2)}) copy-start(f32[768]{0:T(1024)} %copy-done.30) | copy-start | bytes 9220
  434.2 253.9 %reduce-scatter.10.cloned.1.call-start = ((), (), s32[]{:S(2)}) async-start(), calls=%async_computation.11 | async-start | bytes 2359296 | tf_op jit(solution)/shard_map/reduce_scatter | solution.py:239
  434.9 330.8 %reduce-scatter.22.cloned.1.call-start = ((), (), s32[]{:S(2)}) async-start(), calls=%async_computation.19 | async-start | bytes 208896
  442.8 336.4 %all-reduce.21.cloned.1.call-start = ((), (), s32[]{:S(2)}) async-start(), calls=%async_computation.20 | async-start | bytes 1327104 | tf_op jit(solution)/shard_map/psum | solution.py:297
  660.6 191.1 %reduce-scatter.14.cloned.1.call-start = ((), (), s32[]{:S(2)}) async-start(), calls=%async_computation.13 | async-start | bytes 3760128 | tf_op jit(solution)/shard_map/reduce_scatter | solution.py:257
  693.5 2.8 copy-start.22
  693.5 2.9 copy-start.23
  693.5 2.8 copy-start.24
  693.5 2.8 copy-start.29
  693.5 2.8 copy-start.34
  693.5 2.8 copy-start.35
  693.5 64.6 %copy-start.15 = (f32[512]{0:T(512)S(1)}, f32[512]{0:T(512)}, u32[]{:S(2)}) copy-start(f32[512]{0:T(512)} %copy-done.14) | copy-start | bytes 6148
  693.6 64.6 %copy-start.17 = (f32[512]{0:T(512)S(1)}, f32[512]{0:T(512)}, u32[]{:S(2)}) copy-start(f32[512]{0:T(512)} %copy-done.16) | copy-start | bytes 6148
  693.6 66.0 %copy-start.26 = (f32[512]{0:T(512)S(1)}, f32[512]{0:T(512)}, u32[]{:S(2)}) copy-start(f32[512]{0:T(512)} %copy-done.25) | copy-start | bytes 6148
  (15 other events, 21.4 us)
Sparse Core Ops, SparseCore 0:
  10.9 49.8 all-gather.10
  66.6 26.2 all-gather.18
  95.0 27.2 all-gather.20
  125.0 38.3 all-gather.12
  166.1 52.2 all-gather.14
  221.1 51.7 all-gather.16
  415.9 24.6 reduce-scatter.11
  445.2 57.9 reduce-scatter.15
  507.6 74.5 reduce-scatter.17
  585.9 74.5 reduce-scatter.19
  662.9 25.1 reduce-scatter.9
  692.0 53.6 reduce-scatter.21
  748.1 31.0 all-reduce.20
  783.5 68.1 reduce-scatter.13
